TPU v7x, 128 devices: a whole 4x4x4 slice. The times are simulated.
128 devices in a mesh: ctx: 16 (over y_lo, x, core), exp: 8 (over y_hi, z).
Axes of the slice: x: 4, y: 4 (y_hi: 2, y_lo: 2; y = y_hi * 2 + y_lo), z: 4, core: 2. Of those that a mesh axis runs over, the one named last changes fastest.
Arguments:
- queries: bfloat16 [2048, 3072], P('ctx', 'exp'), may hold values from -8 to 8
- keys: bfloat16 [2048, 1024], P('ctx', 'exp'), may hold values from -8 to 8
- values: bfloat16 [2048, 1024], P('ctx', 'exp'), may hold values from -6 to 6
- norm_gain: float32 [3072], replicated, may hold values from 0.1 to 1.9
- routes: int32 [2048, 2], P(('ctx', 'exp')), may hold values from 0 to 7, all different within a row; in each aligned block of 16 rows (0 to 15, 16 to 31, ...) at most 6 rows name the same one
- route_scores: float32 [2048, 2], P(('ctx', 'exp')), may hold values from -8 to 8
- cotangent: bfloat16 [2048, 3072], P(('ctx', 'exp')), may hold values from -6 to 6
- w_gate: bfloat16 [8, 3072, 8192], P('exp', None, 'ctx'), may hold values from -0.109375 to 0.109375
- w_up: bfloat16 [8, 3072, 8192], P('exp', None, 'ctx'), may hold values from -0.109375 to 0.109375
- w_down: bfloat16 [8, 8192, 3072], P('exp', 'ctx'), may hold values from -0.0625 to 0.0625
Outputs:
- mixed: bfloat16 [2048, 3072], P(('ctx', 'exp'))
- grad_input: bfloat16 [2048, 3072], P(('ctx', 'exp'))
- grad_gate: bfloat16 [8, 3072, 8192], P('exp', None, 'ctx')
- grad_up: bfloat16 [8, 3072, 8192], P('exp', None, 'ctx')
- grad_down: bfloat16 [8, 8192, 3072], P('exp', 'ctx')
Inputs may be any that keep to these rules, and one draw needn't show every extreme that they name: `routes`: each row names two different experts. Within each aligned block of 16 rows (the rows of one device) no expert is named by more than 6 rows, a bound that some block reaches.
All inputs are finite; a program needn't handle non-finite values.
Results may differ from a plain program's by a relative error of at most 0.018.
Values may be sent and summed in bfloat16 or wider, within the bound.
A program may use at most 128 MiB of HBM per device.

v0:
```python
import jax
import jax.numpy as jnp
from jax import lax
from jax.sharding import PartitionSpec as P

norm_eps = 1e-05
masked_value = -1e30


def heads_first(query_local, group, head):
    count = query_local.shape[0]
    return query_local.reshape(count, group, head).transpose(1, 0, 2).reshape(group * count, head)


def local(queries, keys, values, norm_gain, routes, route_scores, cotangent, w_gate, w_up, w_down):
    n_exp = lax.axis_size("exp")
    head = keys.shape[1]
    group = queries.shape[1] // head
    tok_ctx = queries.shape[0]
    ctx_index = lax.axis_index("ctx")
    query_flat = heads_first(queries, group, head)
    query_pos = ctx_index * tok_ctx + jnp.tile(jnp.arange(tok_ctx, dtype=jnp.int32), group)
    key_values = lax.all_gather(jnp.concatenate([keys, values], axis=1), "ctx", axis=0, tiled=True)
    scores = lax.dot_general(
        query_flat,
        key_values[:, :head],
        (((1,), (1,)), ((), ())),
        preferred_element_type=jnp.float32,
    ) * head ** (-0.5)
    allowed = jnp.arange(key_values.shape[0], dtype=jnp.int32)[None, :] <= query_pos[:, None]
    scores = jnp.where(allowed, scores, masked_value)
    weights = jnp.exp(scores - jnp.max(scores, axis=1, keepdims=True))
    totals = jnp.sum(weights, axis=1, keepdims=True)
    attended = (
        jnp.dot(
            weights.astype(jnp.bfloat16), key_values[:, head:], preferred_element_type=jnp.float32
        )
        / totals
    )
    attended = (
        attended.reshape(group, tok_ctx, head)
        .transpose(1, 0, 2)
        .reshape(tok_ctx, group * head)
        .astype(jnp.bfloat16)
    )
    features = lax.all_to_all(attended, "exp", split_axis=0, concat_axis=1, tiled=True)
    feats = features.astype(jnp.float32)
    inv_rms = lax.rsqrt(jnp.mean(feats * feats, axis=1) + norm_eps)
    normed = (feats * inv_rms[:, None] * norm_gain[None, :]).astype(jnp.bfloat16)
    tok_dev = normed.shape[0]
    width = normed.shape[1]
    capacity = 3 * tok_dev // n_exp
    slots = n_exp * capacity
    flat_routes = routes.reshape(-1)
    onehot = (flat_routes[:, None] == jnp.arange(n_exp, dtype=jnp.int32)[None, :]).astype(jnp.int32)
    ranks = jnp.sum((jnp.cumsum(onehot, axis=0) - onehot) * onehot, axis=1)
    target = flat_routes * capacity + ranks
    placed = (jnp.arange(slots, dtype=jnp.int32)[:, None] == target[None, :]).astype(jnp.float32)
    place_tokens = placed.reshape(slots, tok_dev, 2).sum(axis=2)
    probs = jax.nn.softmax(route_scores, axis=1)
    mixing = (placed * probs.reshape(-1)[None, :]).reshape(slots, tok_dev, 2).sum(axis=2)
    send = jnp.dot(
        place_tokens.astype(jnp.bfloat16), normed, preferred_element_type=jnp.float32
    ).astype(jnp.bfloat16)
    arrived = lax.all_to_all(
        send.reshape(n_exp, capacity, width), "exp", split_axis=0, concat_axis=0, tiled=True
    ).reshape(slots, width)
    expert_in = lax.all_gather(arrived, "ctx", axis=0, tiled=True)
    gate_w = w_gate[0]
    up_w = w_up[0]
    down_w = w_down[0]
    gate_pre = jnp.dot(expert_in, gate_w, preferred_element_type=jnp.float32)
    up_pre = jnp.dot(expert_in, up_w, preferred_element_type=jnp.float32)
    hidden = (jax.nn.silu(gate_pre) * up_pre).astype(jnp.bfloat16)
    expert_out = lax.psum_scatter(
        jnp.dot(hidden, down_w, preferred_element_type=jnp.float32).astype(jnp.bfloat16),
        "ctx",
        scatter_dimension=0,
        tiled=True,
    )
    returned = lax.all_to_all(
        expert_out.reshape(n_exp, capacity, width), "exp", split_axis=0, concat_axis=0, tiled=True
    ).reshape(slots, width)
    mixed = lax.dot_general(
        mixing,
        returned.astype(jnp.float32),
        (((0,), (0,)), ((), ())),
        precision=lax.Precision.HIGHEST,
    ).astype(jnp.bfloat16)
    grad_slots = jnp.dot(
        mixing, cotangent.astype(jnp.float32), precision=lax.Precision.HIGHEST
    ).astype(jnp.bfloat16)
    grad_arrived = lax.all_to_all(
        grad_slots.reshape(n_exp, capacity, width), "exp", split_axis=0, concat_axis=0, tiled=True
    ).reshape(slots, width)
    grad_out = lax.all_gather(grad_arrived, "ctx", axis=0, tiled=True)
    rows_in = expert_in
    grad_hidden = lax.dot_general(
        grad_out, down_w, (((1,), (1,)), ((), ())), preferred_element_type=jnp.float32
    )
    grad_down = lax.dot_general(
        hidden, grad_out, (((0,), (0,)), ((), ())), preferred_element_type=jnp.float32
    ).astype(jnp.bfloat16)
    sig = jax.nn.sigmoid(gate_pre)
    grad_up_pre = (grad_hidden * (gate_pre * sig)).astype(jnp.bfloat16)
    grad_gate_pre = (grad_hidden * up_pre * sig * (1.0 + gate_pre * (1.0 - sig))).astype(
        jnp.bfloat16
    )
    grad_gate = lax.dot_general(
        rows_in, grad_gate_pre, (((0,), (0,)), ((), ())), preferred_element_type=jnp.float32
    ).astype(jnp.bfloat16)
    grad_upw = lax.dot_general(
        rows_in, grad_up_pre, (((0,), (0,)), ((), ())), preferred_element_type=jnp.float32
    ).astype(jnp.bfloat16)
    term = lax.dot_general(
        grad_gate_pre, gate_w, (((1,), (1,)), ((), ())), preferred_element_type=jnp.float32
    )
    grad_summed = lax.psum_scatter(
        (
            term
            + lax.dot_general(
                grad_up_pre, up_w, (((1,), (1,)), ((), ())), preferred_element_type=jnp.float32
            )
        ).astype(jnp.bfloat16),
        "ctx",
        scatter_dimension=0,
        tiled=True,
    )
    grad_back = lax.all_to_all(
        grad_summed.reshape(n_exp, capacity, width), "exp", split_axis=0, concat_axis=0, tiled=True
    ).reshape(slots, width)
    grad_normed = lax.dot_general(
        place_tokens,
        grad_back.astype(jnp.float32),
        (((0,), (0,)), ((), ())),
        precision=lax.Precision.HIGHEST,
    )
    weighted = grad_normed * norm_gain[None, :]
    inner = jnp.mean(weighted * feats, axis=1)
    grad_input = (inv_rms[:, None] * weighted - feats * (inv_rms**3 * inner)[:, None]).astype(
        jnp.bfloat16
    )
    return (mixed, grad_input, grad_gate[None], grad_upw[None], grad_down[None])


def solution(mesh):
    placed = (
        P("ctx", "exp"),
        P("ctx", "exp"),
        P("ctx", "exp"),
        P(),
        P(("ctx", "exp"), None),
        P(("ctx", "exp"), None),
        P(("ctx", "exp"), None),
        P("exp", None, "ctx"),
        P("exp", None, "ctx"),
        P("exp", "ctx", None),
    )
    return jax.shard_map(
        local,
        mesh=mesh,
        in_specs=placed,
        out_specs=(
            P(("ctx", "exp"), None),
            P(("ctx", "exp"), None),
            P("exp", None, "ctx"),
            P("exp", None, "ctx"),
            P("exp", "ctx", None),
        ),
        check_vma=False,
    )
```

profile of v0, /device:TPU:16, one launch (start us, length us, event | category | flops | bytes accessed | tf_op | source)
XLA Modules:
  0.0 338.5 jit_solution(3207125207926384056)
XLA Ops:
  7.2 1.6 pad_maximum_fusion
  8.8 0.8 copy.35
  9.8 0.2 select_reduce_fusion.1
  10.2 1.0 copy.37
  11.3 0.7 reduce_max.18
  12.0 0.7 fusion.33
  12.7 0.7 fusion.32
  13.4 0.7 multiply_add_fusion
  14.1 30.5 %all-gather.4.cloned.1.call-done = bf16[2048,256]{1,0:T(8,128)(2,1)} async-done(((bf16[128,256]{1,0:T(8,128)(2,1)}), bf16[2048,256]{1,0:T(8,128)(2,1)}) %all-gather.4.cloned.1.call-update) | async-done | bytes 1048592 | tf_op jit(solution)/shard_map/all_gather | solution.py:23
  44.6 1.8 fusion.35
  46.4 0.5 fusion.13
  47.0 0.6 fusion.22
  47.7 0.7 convert_element_type.88
  48.5 7.4 %all-to-all-start = ((bf16[8,16,384]{2,1,0:T(8,128)(2,1)}), bf16[8,16,384]{2,1,0:T(8,128)(2,1)S(1)}, u32[]{:S(2)}, u32[]{:S(2)}) async-start(bf16[8,16,384]{2,1,0:T(8,128)(2,1)} %convert_element_type.88), calls=%async_computation | async-start | bytes 196608 | tf_op jit(solution)/shard_map/all_to_all | solution.py:46
  55.9 5.0 %all-to-all-done = bf16[8,16,384]{2,1,0:T(8,128)(2,1)S(1)} async-done(((bf16[8,16,384]{2,1,0:T(8,128)(2,1)}), bf16[8,16,384]{2,1,0:T(8,128)(2,1)S(1)}, u32[]{:S(2)}, u32[]{:S(2)}) %all-to-all-start) | async-done | bytes 98336 | tf_op jit(solution)/shard_map/all_to_all | solution.py:46
  60.9 0.1 fusion.27
  61.1 1.0 convolution_convert_fusion.5
  62.1 1.8 reshape.111
  63.9 13.6 %all_to_all.30 = bf16[8,6,3072]{2,1,0:T(8,128)(2,1)} all-to-all(bf16[8,6,3072]{2,1,0:T(8,128)(2,1)} %reshape.111), channel_id=1, replica_groups=mesh['ctx'=16,'exp'=8] {'exp'}, dimensions={0} | all-to-all | bytes 589824 | tf_op jit(solution)/shard_map/all_to_all | solution.py:65
  77.5 1.8 reshape.112
  79.4 1.2 convolution_convert_fusion.4
  80.6 1.8 reshape.115
  82.4 18.0 %all_to_all.31 = bf16[8,6,3072]{2,1,0:T(8,128)(2,1)} all-to-all(bf16[8,6,3072]{2,1,0:T(8,128)(2,1)} %reshape.115), channel_id=1, replica_groups=mesh['ctx'=16,'exp'=8] {'exp'}, dimensions={0} | all-to-all | bytes 589824 | tf_op jit(solution)/shard_map/all_to_all | solution.py:93
  100.4 1.8 reshape.116
  102.2 16.1 %all-gather.6.cloned.1.call-done = bf16[768,3072]{1,0:T(8,128)(2,1)} async-done(((bf16[48,3072]{1,0:T(8,128)(2,1)}), bf16[768,3072]{1,0:T(8,128)(2,1)}) %all-gather.6.cloned.1.call-update) | async-done | bytes 4718608 | tf_op jit(solution)/shard_map/all_gather | solution.py:68
  118.4 7.2 %fusion.7 = f32[768,512]{1,0:T(8,128)} fusion(bf16[768,3072]{1,0:T(8,128)(2,1)} %all-gather.6.cloned.1.call-done, bf16[1,3072,512]{2,1,0:T(8,128)(2,1)} %param.18), kind=kOutput, calls=%fused_computation.16 | convolution fusion | flops 2415919104 | bytes 9437184 | tf_op jit(solution)/shard_map/dot_general | solution.py:73
  125.6 3.7 %fusion.11 = f32[768,512]{1,0:T(8,128)} fusion(bf16[768,3072]{1,0:T(8,128)(2,1)S(1)} %copy-done.6, bf16[1,3072,512]{2,1,0:T(8,128)(2,1)S(1)} %copy-done.7), kind=kOutput, calls=%fused_computation.20 | convolution fusion | flops 2415919104 | bytes 9437184 | tf_op jit(solution)/shard_map/dot_general | solution.py:72
  129.3 30.0 %all-gather.8.cloned.1.call-done = bf16[768,3072]{1,0:T(8,128)(2,1)} async-done(((bf16[48,3072]{1,0:T(8,128)(2,1)}), bf16[768,3072]{1,0:T(8,128)(2,1)}) %all-gather.8.cloned.1.call-update) | async-done | bytes 4718608 | tf_op jit(solution)/shard_map/all_gather | solution.py:96
  159.3 7.0 %multiply_convert_fusion = (bf16[768,512]{1,0:T(8,128)(2,1)}, bf16[768,512]{1,0:T(8,128)(2,1)}, bf16[768,512]{1,0:T(8,128)(2,1)S(1)}) fusion(f32[768,512]{1,0:T(8,128)} %fusion.11, f32[768,512]{1,0:T(8,128)} %fusion.7, bf16[768,3072]{1,0:T(8,128)(2,1)} %all-gather.8.cloned.1.call-done, bf16[1,512,3072]{2,1,0:T(8,128)(2,1)S(1)} %copy-done), kind=kOutput, calls=%fused_computation.28 | convolution fusion | flops 2421817344 | bytes 13369344 | tf_op jit(solution)/shard_map/dot_general | solution.py:98
  166.3 0.9 copy-done.8
  167.2 4.2 %convolution_convert_fusion = bf16[768,3072]{1,0:T(8,128)(2,1)} fusion(bf16[768,512]{1,0:T(8,128)(2,1)S(1)} %get-tuple-element.9, bf16[1,512,3072]{2,1,0:T(8,128)(2,1)S(1)} %copy-done), kind=kOutput, calls=%fused_computation.1 | convolution fusion | flops 2418278400 | bytes 8650752 | tf_op jit(solution)/shard_map/dot_general | solution.py:76
  171.5 0.2 reduce-scatter.5.cloned.1.call-start
  171.7 4.9 %fusion.9 = f32[768,3072]{1,0:T(8,128)S(1)} fusion(bf16[768,512]{1,0:T(8,128)(2,1)} %get-tuple-element.8, bf16[1,3072,512]{2,1,0:T(8,128)(2,1)} %param.17), kind=kOutput, calls=%fused_computation.18 | convolution fusion | flops 2415919104 | bytes 13369344 | tf_op jit(solution)/shard_map/dot_general | solution.py:115
  176.6 4.4 %add_convert_fusion = bf16[768,3072]{1,0:T(8,128)(2,1)} fusion(f32[768,3072]{1,0:T(8,128)S(1)} %fusion.9, bf16[768,512]{1,0:T(8,128)(2,1)S(1)} %copy-done.2, bf16[1,3072,512]{2,1,0:T(8,128)(2,1)S(1)} %copy-done.1), kind=kOutput, calls=%fused_computation | convolution fusion | flops 2420637696 | bytes 18087936 | tf_op jit(solution)/shard_map/dot_general | solution.py:121
  181.1 6.9 %fusion.2 = bf16[1,512,3072]{2,1,0:T(8,128)(2,1)} fusion(bf16[768,512]{1,0:T(8,128)(2,1)} %copy-done.8, bf16[768,3072]{1,0:T(8,128)(2,1)} %all-gather.8.cloned.1.call-done), kind=kOutput, calls=%fused_computation.7 | convolution fusion | flops 2417491968 | bytes 8650752 | tf_op jit(solution)/shard_map/dot_general | solution.py:101
  188.0 51.4 %reduce-scatter.3.cloned.1.call-done = bf16[48,3072]{1,0:T(8,128)(2,1)} async-done(((bf16[768,3072]{1,0:T(8,128)(2,1)}), bf16[48,3072]{1,0:T(8,128)(2,1)}) %reduce-scatter.3.cloned.1.call-update) | async-done | bytes 294928 | tf_op jit(solution)/shard_map/reduce_scatter | solution.py:75
  239.4 1.8 reshape.113
  241.2 7.5 %all-to-all-start.2 = ((bf16[8,6,3072]{2,1,0:T(8,128)(2,1)}), bf16[8,6,3072]{2,1,0:T(8,128)(2,1)}, u32[]{:S(2)}, u32[]{:S(2)}) async-start(bf16[8,6,3072]{2,1,0:T(8,128)(2,1)} %reshape.113), calls=%async_computation.3 | async-start | bytes 786432 | tf_op jit(solution)/shard_map/all_to_all | solution.py:81
  248.7 7.0 %fusion.1 = bf16[1,3072,512]{2,1,0:T(8,128)(2,1)} fusion(bf16[768,3072]{1,0:T(8,128)(2,1)} %all-gather.6.cloned.1.call-done, bf16[768,512]{1,0:T(8,128)(2,1)} %get-tuple-element.7), kind=kOutput, calls=%fused_computation.6 | convolution fusion | flops 2417491968 | bytes 8650752 | tf_op jit(solution)/shard_map/dot_general | solution.py:112
  255.7 52.4 %reduce-scatter.5.cloned.1.call-done = bf16[48,3072]{1,0:T(8,128)(2,1)} async-done(((bf16[768,3072]{1,0:T(8,128)(2,1)}), bf16[48,3072]{1,0:T(8,128)(2,1)}) %reduce-scatter.5.cloned.1.call-update) | async-done | bytes 294928 | tf_op jit(solution)/shard_map/reduce_scatter | solution.py:118
  308.2 1.8 reshape.117
  310.0 7.5 %all-to-all-start.4 = ((bf16[8,6,3072]{2,1,0:T(8,128)(2,1)}), bf16[8,6,3072]{2,1,0:T(8,128)(2,1)}, u32[]{:S(2)}, u32[]{:S(2)}) async-start(bf16[8,6,3072]{2,1,0:T(8,128)(2,1)} %reshape.117), calls=%async_computation.6 | async-start | bytes 786432 | tf_op jit(solution)/shard_map/all_to_all | solution.py:129
  317.5 6.9 %fusion = bf16[1,3072,512]{2,1,0:T(8,128)(2,1)} fusion(bf16[768,3072]{1,0:T(8,128)(2,1)} %all-gather.6.cloned.1.call-done, bf16[768,512]{1,0:T(8,128)(2,1)} %get-tuple-element.8), kind=kOutput, calls=%fused_computation.5 | convolution fusion | flops 2417491968 | bytes 8650752 | tf_op jit(solution)/shard_map/dot_general | solution.py:109
  324.4 1.8 reshape.114
  326.2 1.9 convolution_convert_fusion.6
  328.1 1.8 reshape.118
  329.9 1.3 multiply_reduce_fusion
  331.2 0.7 subtract_convert_fusion
  (41 shorter events, 1.0 us)
Async XLA Ops:
  7.2 152.1 %copy-start = (bf16[1,512,3072]{2,1,0:T(8,128)(2,1)S(1)}, bf16[1,512,3072]{2,1,0:T(8,128)(2,1)}, u32[]{:S(2)}) copy-start(bf16[1,512,3072]{2,1,0:T(8,128)(2,1)} %param.19) | copy-start | bytes 9437188
  7.2 37.5 %all-gather.4.cloned.1.call-start = ((), (), s32[]{:S(2)}) async-start(), calls=%async_computation.7 | async-start | bytes 1114112 | tf_op jit(solution)/shard_map/all_gather | solution.py:23
  44.6 2.3 copy-start.3
  47.0 14.1 %copy-start.5 = (f32[3072]{0:T(1024)S(1)}, f32[3072]{0:T(1024)}, u32[]{:S(2)}) copy-start(f32[3072]{0:T(1024)} %param.13) | copy-start | bytes 36868
  47.6 31.8 %copy-start.4 = (bf16[16,3072]{1,0:T(8,128)(2,1)S(1)}, bf16[16,3072]{1,0:T(8,128)(2,1)}, u32[]{:S(2)}) copy-start(bf16[16,3072]{1,0:T(8,128)(2,1)} %param.16) | copy-start | bytes 294916
  48.5 12.5 %all-to-all-start = ((bf16[8,16,384]{2,1,0:T(8,128)(2,1)}), bf16[8,16,384]{2,1,0:T(8,128)(2,1)S(1)}, u32[]{:S(2)}, u32[]{:S(2)}) async-start(bf16[8,16,384]{2,1,0:T(8,128)(2,1)} %convert_element_type.88), calls=%async_computation | async-start | bytes 196608 | tf_op jit(solution)/shard_map/all_to_all | solution.py:46
  55.9 62.5 %all-gather.6.cloned.1.call-start = ((), (), s32[]{:S(2)}) async-start(), calls=%async_computation.8 | async-start | bytes 5013504 | tf_op jit(solution)/shard_map/all_gather | solution.py:68
  79.4 80.0 %all-gather.8.cloned.1.call-start = ((), (), s32[]{:S(2)}) async-start(), calls=%async_computation.10 | async-start | bytes 5013504 | tf_op jit(solution)/shard_map/all_gather | solution.py:96
  102.2 137.2 %reduce-scatter.3.cloned.1.call-start = ((), (), s32[]{:S(2)}) async-start(), calls=%async_computation.9 | async-start | bytes 5013504 | tf_op jit(solution)/shard_map/reduce_scatter | solution.py:75
  118.4 7.2 %copy-start.6 = (bf16[768,3072]{1,0:T(8,128)(2,1)S(1)}, bf16[768,3072]{1,0:T(8,128)(2,1)}, u32[]{:S(2)}) copy-start(bf16[768,3072]{1,0:T(8,128)(2,1)} %all-gather.6.cloned.1.call-done) | copy-start | bytes 14155780
  118.4 7.2 %copy-start.7 = (bf16[1,3072,512]{2,1,0:T(8,128)(2,1)S(1)}, bf16[1,3072,512]{2,1,0:T(8,128)(2,1)}, u32[]{:S(2)}) copy-start(bf16[1,3072,512]{2,1,0:T(8,128)(2,1)} %param.17) | copy-start | bytes 9437188
  166.3 0.9 copy-start.8
  171.5 136.7 %reduce-scatter.5.cloned.1.call-start = ((), (), s32[]{:S(2)}) async-start(), calls=%async_computation.11 | async-start | bytes 5013504 | tf_op jit(solution)/shard_map/reduce_scatter | solution.py:118
  171.7 4.9 %copy-start.1 = (bf16[1,3072,512]{2,1,0:T(8,128)(2,1)S(1)}, bf16[1,3072,512]{2,1,0:T(8,128)(2,1)}, u32[]{:S(2)}) copy-start(bf16[1,3072,512]{2,1,0:T(8,128)(2,1)} %param.18) | copy-start | bytes 9437188
  171.7 4.9 %copy-start.2 = (bf16[768,512]{1,0:T(8,128)(2,1)S(1)}, bf16[768,512]{1,0:T(8,128)(2,1)}, u32[]{:S(2)}) copy-start(bf16[768,512]{1,0:T(8,128)(2,1)} %get-tuple-element.7) | copy-start | bytes 2359300
  241.2 68.8 %all-to-all-start.2 = ((bf16[8,6,3072]{2,1,0:T(8,128)(2,1)}), bf16[8,6,3072]{2,1,0:T(8,128)(2,1)}, u32[]{:S(2)}, u32[]{:S(2)}) async-start(bf16[8,6,3072]{2,1,0:T(8,128)(2,1)} %reshape.113), calls=%async_computation.3 | async-start | bytes 786432 | tf_op jit(solution)/shard_map/all_to_all | solution.py:81
  310.0 18.1 %all-to-all-start.4 = ((bf16[8,6,3072]{2,1,0:T(8,128)(2,1)}), bf16[8,6,3072]{2,1,0:T(8,128)(2,1)}, u32[]{:S(2)}, u32[]{:S(2)}) async-start(bf16[8,6,3072]{2,1,0:T(8,128)(2,1)} %reshape.117), calls=%async_computation.6 | async-start | bytes 786432 | tf_op jit(solution)/shard_map/all_to_all | solution.py:129
Sparse Core Ops, SparseCore 0:
  10.3 34.3 all-gather.3
  79.5 38.8 all-gather.5
  120.7 38.6 all-gather.7
  171.6 67.7 reduce-scatter.2
  241.6 66.4 reduce-scatter.4
where the time goes:
time: 340 us; the launch traced here: 338 us
  waiting for transfers between devices  186 us (55%)
  matrix products  60 us (18%)
  blocking collectives  31.6 us (9%)
  starting transfers between devices  22.8 us (7%)
  local copies, waits for them, and re-layouts  18.4 us (5%)
  between operations  13.9 us (4%)
  other arithmetic  6.2 us (2%)
    reduce_scatter x1, waiting for transfers between devices, local(): lax.psum_scatter((term + lax.dot_general(grad_up_pre, up_w, (((1,), (1,))...  52.4 us
    reduce_scatter x1, waiting for transfers between devices, local(): lax.psum_scatter(jnp.dot(hidden, down_w, preferred_element_type=jnp.float...  51.4 us
    all_gather x1, waiting for transfers between devices, local(): lax.all_gather(jnp.concatenate([keys, values], axis=1), 'ctx', axis=0, ti...  30.5 us
    all_gather x1, waiting for transfers between devices, local(): grad_out = lax.all_gather(grad_arrived, 'ctx', axis=0, tiled=True)  30 us
    all_to_all x1, blocking collectives, local(): lax.all_to_all(grad_slots.reshape(n_exp, capacity, width), 'exp', split_a...  18 us
    all_gather x1, waiting for transfers between devices, local(): expert_in = lax.all_gather(arrived, 'ctx', axis=0, tiled=True)  16.1 us
    all_to_all x1, blocking collectives, local(): lax.all_to_all(send.reshape(n_exp, capacity, width), 'exp', split_axis=0,...  13.6 us
    all_to_all x1, starting transfers between devices, local(): lax.all_to_all(grad_summed.reshape(n_exp, capacity, width), 'exp', split_...  7.52 us
  transfers between devices with their start and end apart: 8, of which 6 were waited for; matrix products, arithmetic and copies ran while one was open for 17% of the time, Pallas kernels for 0%

commit v1 on v0

--- a/solution.py
+++ b/solution.py
@@ -65,7 +65,8 @@
     arrived = lax.all_to_all(
         send.reshape(n_exp, capacity, width), "exp", split_axis=0, concat_axis=0, tiled=True
     ).reshape(slots, width)
-    expert_in = lax.all_gather(arrived, "ctx", axis=0, tiled=True)
+    stack = jnp.stack([arrived] * lax.axis_size("ctx"))
+    expert_in = jnp.concatenate(lax.all_to_all(stack, "ctx", 0, 0), axis=0)
     gate_w = w_gate[0]
     up_w = w_up[0]
     down_w = w_down[0]

time: 340 us -> 329 us (0.968)
  waiting for transfers between devices: 186 us -> 110 us
  blocking collectives: 31.6 us -> 106 us
  starting transfers between devices: 22.8 us -> 15.1 us
    all_to_all x0 -> x2, blocking collectives: none -> 71.4 us  [the longest x1 59.2 us: local(): expert_in = jnp.concatenate(lax.all_to_all(stack, 'ctx', 0, 0), axis=0)]
    all_gather x1, waiting for transfers between devices: 30 us -> 0.01 us  [local(): grad_out = lax.all_gather(grad_arrived, 'ctx', axis=0, tiled=True)]
    all_gather x1, waiting for transfers between devices: 30.5 us -> 9.34 us  [local(): lax.all_gather(jnp.concatenate([keys, values], axis=1), 'ctx', axis=0, ti...]
    all_gather x1 -> x0, waiting for transfers between devices: 16.1 us -> none  [local(): expert_in = lax.all_gather(arrived, 'ctx', axis=0, tiled=True)]
    all_to_all x1 -> x0, starting transfers between devices: 7.39 us -> none  [local(): lax.all_to_all(attended, 'exp', split_axis=0, concat_axis=1, tiled=True)]
    all_to_all x1 -> x0, waiting for transfers between devices: 5 us -> none  [local(): lax.all_to_all(attended, 'exp', split_axis=0, concat_axis=1, tiled=True)]
    all_to_all x1, blocking collectives: 13.6 us -> 18.5 us  [local(): lax.all_to_all(send.reshape(n_exp, capacity, width), 'exp', split_axis=0,...]
    reduce_scatter x1, waiting for transfers between devices: 51.4 us -> 47.6 us  [local(): lax.psum_scatter(jnp.dot(hidden, down_w, preferred_element_type=jnp.float...]
  transfers between devices with their start and end apart: 8 -> 6, of which waited for: 6 -> 3; matrix products, arithmetic and copies ran while one was open for 17% -> 19% of each run, Pallas kernels for 0% -> 0%
where the time goes in v1:
time: 329 us; the launch traced here: 328 us
  waiting for transfers between devices  110 us (33%)
  blocking collectives  106 us (32%)
  matrix products  56.8 us (17%)
  local copies, waits for them, and re-layouts  19.7 us (6%)
  starting transfers between devices  15.1 us (5%)
  between operations  13.9 us (4%)
  other arithmetic  6.21 us (2%)
    all_to_all x1, blocking collectives, local(): expert_in = jnp.concatenate(lax.all_to_all(stack, 'ctx', 0, 0), axis=0)  59.2 us
    reduce_scatter x1, waiting for transfers between devices, local(): lax.psum_scatter((term + lax.dot_general(grad_up_pre, up_w, (((1,), (1,))...  52.9 us
    reduce_scatter x1, waiting for transfers between devices, local(): lax.psum_scatter(jnp.dot(hidden, down_w, preferred_element_type=jnp.float...  47.6 us
    all_to_all x1, blocking collectives, local(): lax.all_to_all(send.reshape(n_exp, capacity, width), 'exp', split_axis=0,...  18.5 us
    all_to_all x1, blocking collectives, local(): lax.all_to_all(grad_slots.reshape(n_exp, capacity, width), 'exp', split_a...  16.4 us
    all_to_all x1, blocking collectives, local(): lax.all_to_all(attended, 'exp', split_axis=0, concat_axis=1, tiled=True)  12.2 us
    all_gather x1, waiting for transfers between devices, local(): lax.all_gather(jnp.concatenate([keys, values], axis=1), 'ctx', axis=0, ti...  9.34 us
    all_to_all x1, starting transfers between devices, local(): lax.all_to_all(expert_out.reshape(n_exp, capacity, width), 'exp', split_a...  7.41 us
  transfers between devices with their start and end apart: 6, of which 3 were waited for; matrix products, arithmetic and copies ran while one was open for 19% of the time, Pallas kernels for 0%

profile of v1, /device:TPU:16, one launch (start us, length us, event | category | flops | bytes accessed | tf_op | source)
XLA Modules:
  0.0 328.1 jit_solution(2335261034715704574)
XLA Ops:
  7.2 1.6 pad_maximum_fusion
  8.9 0.8 copy.35
  9.8 0.2 select_reduce_fusion.1
  10.2 0.7 reduce_max.18
  10.9 0.7 fusion.33
  11.6 0.7 fusion.32
  12.3 0.7 multiply_add_fusion
  13.1 2.0 convolution_convert_fusion.4
  15.1 1.1 reshape.117
  16.2 16.4 %all_to_all.35 = bf16[8,6,3072]{2,1,0:T(8,128)(2,1)} all-to-all(bf16[8,6,3072]{2,1,0:T(8,128)(2,1)S(1)} %reshape.117), channel_id=1, replica_groups=mesh['ctx'=16,'exp'=8] {'exp'}, dimensions={0} | all-to-all | bytes 589824 | tf_op jit(solution)/shard_map/all_to_all | solution.py:94
  32.6 1.8 reshape.118
  34.5 1.0 copy.37
  35.5 0.1 copy.38
  35.7 9.3 %all-gather.3.cloned.1.call-done = bf16[2048,256]{1,0:T(8,128)(2,1)} async-done(((bf16[128,256]{1,0:T(8,128)(2,1)}), bf16[2048,256]{1,0:T(8,128)(2,1)}) %all-gather.3.cloned.1.call-update) | async-done | bytes 1048592 | tf_op jit(solution)/shard_map/all_gather | solution.py:23
  45.0 1.8 fusion.35
  46.8 0.5 fusion.13
  47.4 0.6 fusion.22
  48.2 12.2 %all_to_all.36 = bf16[8,16,384]{2,1,0:T(8,128)(2,1)S(1)} all-to-all(bf16[8,16,384]{2,1,0:T(8,128)(2,1)S(1)} %convert_element_type.88), channel_id=1, replica_groups=mesh['ctx'=16,'exp'=8] {'exp'}, dimensions={0} | all-to-all | bytes 196608 | tf_op jit(solution)/shard_map/all_to_all | solution.py:46
  60.4 0.1 fusion.27
  60.6 1.0 convolution_convert_fusion.5
  61.6 1.8 reshape.113
  63.4 18.5 %all_to_all.37 = bf16[8,6,3072]{2,1,0:T(8,128)(2,1)} all-to-all(bf16[8,6,3072]{2,1,0:T(8,128)(2,1)} %reshape.113), channel_id=1, replica_groups=mesh['ctx'=16,'exp'=8] {'exp'}, dimensions={0} | all-to-all | bytes 589824 | tf_op jit(solution)/shard_map/all_to_all | solution.py:65
  81.9 1.8 stack_reshape.2
  83.8 1.5 stack.3
  85.3 59.2 %all_to_all.38 = bf16[16,48,3072]{2,1,0:T(8,128)(2,1)S(1)} all-to-all(bf16[16,48,3072]{2,1,0:T(8,128)(2,1)S(1)} %stack.3), channel_id=1, replica_groups=mesh['ctx'=16,'exp'=8] {'ctx'}, dimensions={0} | all-to-all | bytes 9437184 | tf_op jit(solution)/shard_map/all_to_all | solution.py:69
  144.5 3.7 %fusion.7 = f32[768,512]{1,0:T(8,128)} fusion(bf16[768,3072]{1,0:T(8,128)(2,1)S(1)} %bitcast.59, bf16[1,3072,512]{2,1,0:T(8,128)(2,1)S(1)} %copy-done.3), kind=kOutput, calls=%fused_computation.16 | convolution fusion | flops 2415919104 | bytes 9437184 | tf_op jit(solution)/shard_map/dot_general | solution.py:74
  148.2 3.7 %fusion.11 = f32[768,512]{1,0:T(8,128)} fusion(bf16[768,3072]{1,0:T(8,128)(2,1)S(1)} %bitcast.60, bf16[1,3072,512]{2,1,0:T(8,128)(2,1)S(1)} %copy-done.9), kind=kOutput, calls=%fused_computation.20 | convolution fusion | flops 2415919104 | bytes 9437184 | tf_op jit(solution)/shard_map/dot_general | solution.py:73
  152.0 7.0 %multiply_convert_fusion = (bf16[768,512]{1,0:T(8,128)(2,1)}, bf16[768,512]{1,0:T(8,128)(2,1)}, bf16[768,512]{1,0:T(8,128)(2,1)S(1)}) fusion(f32[768,512]{1,0:T(8,128)} %fusion.11, f32[768,512]{1,0:T(8,128)} %fusion.7, bf16[768,3072]{1,0:T(8,128)(2,1)} %all-gather.5.cloned.1.call-done, bf16[1,512,3072]{2,1,0:T(8,128)(2,1)S(1)} %copy-done), kind=kOutput, calls=%fused_computation.28 | convolution fusion | flops 2421817344 | bytes 13369344 | tf_op jit(solution)/shard_map/dot_general | solution.py:99
  159.0 0.9 copy-done.11
  159.9 4.2 %convolution_convert_fusion = bf16[768,3072]{1,0:T(8,128)(2,1)} fusion(bf16[768,512]{1,0:T(8,128)(2,1)S(1)} %get-tuple-element.9, bf16[1,512,3072]{2,1,0:T(8,128)(2,1)S(1)} %copy-done), kind=kOutput, calls=%fused_computation.1 | convolution fusion | flops 2418278400 | bytes 8650752 | tf_op jit(solution)/shard_map/dot_general | solution.py:77
  164.1 0.2 reduce-scatter.5.cloned.1.call-start
  164.4 4.9 %fusion.9 = f32[768,3072]{1,0:T(8,128)S(1)} fusion(bf16[768,512]{1,0:T(8,128)(2,1)} %get-tuple-element.8, bf16[1,3072,512]{2,1,0:T(8,128)(2,1)} %param.17), kind=kOutput, calls=%fused_computation.18 | convolution fusion | flops 2415919104 | bytes 13369344 | tf_op jit(solution)/shard_map/dot_general | solution.py:116
  169.3 4.4 %add_convert_fusion = bf16[768,3072]{1,0:T(8,128)(2,1)} fusion(f32[768,3072]{1,0:T(8,128)S(1)} %fusion.9, bf16[768,512]{1,0:T(8,128)(2,1)S(1)} %copy-done.5, bf16[1,3072,512]{2,1,0:T(8,128)(2,1)S(1)} %copy-done.4), kind=kOutput, calls=%fused_computation | convolution fusion | flops 2420637696 | bytes 18087936 | tf_op jit(solution)/shard_map/dot_general | solution.py:122
  173.8 1.1 copy-done.6
  174.9 6.6 %fusion.1 = bf16[1,3072,512]{2,1,0:T(8,128)(2,1)} fusion(bf16[768,3072]{1,0:T(8,128)(2,1)} %bitcast.61, bf16[768,512]{1,0:T(8,128)(2,1)S(1)} %copy-done.6), kind=kOutput, calls=%fused_computation.6 | convolution fusion | flops 2417491968 | bytes 8650752 | tf_op jit(solution)/shard_map/dot_general | solution.py:113
  181.4 47.6 %reduce-scatter.3.cloned.1.call-done = bf16[48,3072]{1,0:T(8,128)(2,1)} async-done(((bf16[768,3072]{1,0:T(8,128)(2,1)}), bf16[48,3072]{1,0:T(8,128)(2,1)}) %reduce-scatter.3.cloned.1.call-update) | async-done | bytes 294928 | tf_op jit(solution)/shard_map/reduce_scatter | solution.py:76
  229.1 1.8 reshape.115
  230.9 7.4 %all-to-all-start.3 = ((bf16[8,6,3072]{2,1,0:T(8,128)(2,1)}), bf16[8,6,3072]{2,1,0:T(8,128)(2,1)}, u32[]{:S(2)}, u32[]{:S(2)}) async-start(bf16[8,6,3072]{2,1,0:T(8,128)(2,1)} %reshape.115), calls=%async_computation.4 | async-start | bytes 786432 | tf_op jit(solution)/shard_map/all_to_all | solution.py:82
  238.3 6.6 %fusion = bf16[1,3072,512]{2,1,0:T(8,128)(2,1)} fusion(bf16[768,3072]{1,0:T(8,128)(2,1)} %bitcast.62, bf16[768,512]{1,0:T(8,128)(2,1)S(1)} %copy-done.10), kind=kOutput, calls=%fused_computation.5 | convolution fusion | flops 2417491968 | bytes 8650752 | tf_op jit(solution)/shard_map/dot_general | solution.py:110
  244.9 52.9 %reduce-scatter.5.cloned.1.call-done = bf16[48,3072]{1,0:T(8,128)(2,1)} async-done(((bf16[768,3072]{1,0:T(8,128)(2,1)}), bf16[48,3072]{1,0:T(8,128)(2,1)}) %reduce-scatter.5.cloned.1.call-update) | async-done | bytes 294928 | tf_op jit(solution)/shard_map/reduce_scatter | solution.py:119
  297.7 1.8 reshape.119
  299.6 7.4 %all-to-all-start.5 = ((bf16[8,6,3072]{2,1,0:T(8,128)(2,1)}), bf16[8,6,3072]{2,1,0:T(8,128)(2,1)}, u32[]{:S(2)}, u32[]{:S(2)}) async-start(bf16[8,6,3072]{2,1,0:T(8,128)(2,1)} %reshape.119), calls=%async_computation.7 | async-start | bytes 786432 | tf_op jit(solution)/shard_map/all_to_all | solution.py:130
  306.9 7.0 %fusion.2 = bf16[1,512,3072]{2,1,0:T(8,128)(2,1)} fusion(bf16[768,512]{1,0:T(8,128)(2,1)} %copy-done.11, bf16[768,3072]{1,0:T(8,128)(2,1)} %all-gather.5.cloned.1.call-done), kind=kOutput, calls=%fused_computation.7 | convolution fusion | flops 2417491968 | bytes 8650752 | tf_op jit(solution)/shard_map/dot_general | solution.py:102
  314.0 1.8 reshape.116
  315.8 1.9 convolution_convert_fusion.6
  317.6 1.8 reshape.120
  319.4 1.3 multiply_reduce_fusion
  320.8 0.7 subtract_convert_fusion
  (45 shorter events, 0.9 us)
Async XLA Ops:
  7.2 144.8 %copy-start = (bf16[1,512,3072]{2,1,0:T(8,128)(2,1)S(1)}, bf16[1,512,3072]{2,1,0:T(8,128)(2,1)}, u32[]{:S(2)}) copy-start(bf16[1,512,3072]{2,1,0:T(8,128)(2,1)} %param.19) | copy-start | bytes 9437188
  7.2 37.8 %all-gather.3.cloned.1.call-start = ((), (), s32[]{:S(2)}) async-start(), calls=%async_computation.8 | async-start | bytes 1114112 | tf_op jit(solution)/shard_map/all_gather | solution.py:23
  8.8 143.1 %all-gather.5.cloned.1.call-start = ((), (), s32[]{:S(2)}) async-start(), calls=%async_computation.10 | async-start | bytes 5013504 | tf_op jit(solution)/shard_map/all_gather | solution.py:97
  34.5 194.6 %reduce-scatter.3.cloned.1.call-start = ((), (), s32[]{:S(2)}) async-start(), calls=%async_computation.9 | async-start | bytes 5013504 | tf_op jit(solution)/shard_map/reduce_scatter | solution.py:76
  45.0 2.3 copy-start.7
  47.4 13.2 %copy-start.8 = (f32[3072]{0:T(1024)S(1)}, f32[3072]{0:T(1024)}, u32[]{:S(2)}) copy-start(f32[3072]{0:T(1024)} %param.13) | copy-start | bytes 36868
  85.3 59.2 %copy-start.3 = (bf16[1,3072,512]{2,1,0:T(8,128)(2,1)S(1)}, bf16[1,3072,512]{2,1,0:T(8,128)(2,1)}, u32[]{:S(2)}) copy-start(bf16[1,3072,512]{2,1,0:T(8,128)(2,1)} %param.18) | copy-start | bytes 9437188
  144.5 3.7 %copy-start.2 = (bf16[16,48,3072]{2,1,0:T(8,128)(2,1)}, bf16[16,48,3072]{2,1,0:T(8,128)(2,1)S(1)}, u32[]{:S(2)}) copy-start(bf16[16,48,3072]{2,1,0:T(8,128)(2,1)S(1)} %all_to_all.38) | copy-start | bytes 14155780
  144.5 3.7 %copy-start.9 = (bf16[1,3072,512]{2,1,0:T(8,128)(2,1)S(1)}, bf16[1,3072,512]{2,1,0:T(8,128)(2,1)}, u32[]{:S(2)}) copy-start(bf16[1,3072,512]{2,1,0:T(8,128)(2,1)} %param.17) | copy-start | bytes 9437188
  159.0 0.9 copy-start.11
  164.1 133.6 %reduce-scatter.5.cloned.1.call-start = ((), (), s32[]{:S(2)}) async-start(), calls=%async_computation.11 | async-start | bytes 5013504 | tf_op jit(solution)/shard_map/reduce_scatter | solution.py:119
  164.4 4.9 %copy-start.4 = (bf16[1,3072,512]{2,1,0:T(8,128)(2,1)S(1)}, bf16[1,3072,512]{2,1,0:T(8,128)(2,1)}, u32[]{:S(2)}) copy-start(bf16[1,3072,512]{2,1,0:T(8,128)(2,1)} %param.18) | copy-start | bytes 9437188
  164.4 4.9 %copy-start.5 = (bf16[768,512]{1,0:T(8,128)(2,1)S(1)}, bf16[768,512]{1,0:T(8,128)(2,1)}, u32[]{:S(2)}) copy-start(bf16[768,512]{1,0:T(8,128)(2,1)} %get-tuple-element.7) | copy-start | bytes 2359300
  173.7 1.1 copy-start.6
  174.9 63.4 %copy-start.10 = (bf16[768,512]{1,0:T(8,128)(2,1)S(1)}, bf16[768,512]{1,0:T(8,128)(2,1)}, u32[]{:S(2)}) copy-start(bf16[768,512]{1,0:T(8,128)(2,1)} %get-tuple-element.8) | copy-start | bytes 2359300
  230.9 68.7 %all-to-all-start.3 = ((bf16[8,6,3072]{2,1,0:T(8,128)(2,1)}), bf16[8,6,3072]{2,1,0:T(8,128)(2,1)}, u32[]{:S(2)}, u32[]{:S(2)}) async-start(bf16[8,6,3072]{2,1,0:T(8,128)(2,1)} %reshape.115), calls=%async_computation.4 | async-start | bytes 786432 | tf_op jit(solution)/shard_map/all_to_all | solution.py:82
  299.6 18.1 %all-to-all-start.5 = ((bf16[8,6,3072]{2,1,0:T(8,128)(2,1)}), bf16[8,6,3072]{2,1,0:T(8,128)(2,1)}, u32[]{:S(2)}, u32[]{:S(2)}) async-start(bf16[8,6,3072]{2,1,0:T(8,128)(2,1)} %reshape.119), calls=%async_computation.7 | async-start | bytes 786432 | tf_op jit(solution)/shard_map/all_to_all | solution.py:130
  306.9 14.6 %copy-start.1 = (bf16[1,512,3072]{2,1,0:T(8,128)(2,1)S(1)}, bf16[1,512,3072]{2,1,0:T(8,128)(2,1)}, u32[]{:S(2)}) copy-start(bf16[1,512,3072]{2,1,0:T(8,128)(2,1)} %param.19) | copy-start | bytes 9437188
Sparse Core Ops, SparseCore 0:
  10.3 34.6 all-gather.2
  47.3 41.7 all-gather.4
  164.3 64.7 reduce-scatter.2
  231.3 66.3 reduce-scatter.4
